TPU v7x, 32 devices: a whole 2x2x4 slice. The times are simulated.
32 devices in a mesh: view: 2 (over core), dom: 16 (over z, y, x).
Axes of the slice: x: 2, y: 2, z: 4, core: 2. Of those that a mesh axis runs over, the one named last changes fastest.
Arguments:
- features: bfloat16 [16384, 512], P('dom'), may hold values from -6 to 6
- feat_keep: int32 [2, 512], P('view'), may hold values 0 or 1
- w_first: bfloat16 [512, 512], replicated, may hold values from -0.25 to 0.25
- w_second: bfloat16 [512, 512], replicated, may hold values from -0.25 to 0.25
- adjacency: bfloat16 [2, 1024, 128, 128], P('view', 'dom'), may hold values from 0 to 0.015625
- tile_src: int32 [2, 128, 8], P('view', 'dom'), may hold values from 0 to 8, as said below
- halo_rows: int32 [16, 16, 8], P('dom'), may hold values from 0 to 1023
- halo_live: int32 [16, 16], P('dom'), may hold values from 0 to 8, as said below
- neg_pick: int32 [16, 16, 8], P('dom'), may hold values from 0 to 1023
Outputs:
- node_loss: float32 [2, 16384], P('view', 'dom')
- grad_first: float32 [512, 512], replicated
- grad_second: float32 [512, 512], replicated
Inputs may be any that keep to these rules, and one draw needn't show every extreme that they name: `tile_src`: the last tile of the first block of every partition reads its last halo block. `halo_live`: some receiver gets 8 live rows from every sender.
All inputs are finite; a program needn't handle non-finite values. No bound on the sum of `feat_keep` on one device may be relied on, other than what follows from the above.
Results may differ from a plain program's by a relative error of at most 0.0015.
The roundings to bfloat16 on the way count: a program that leaves them out, or rounds other values in their place, can miss the bound.
Values may be sent and summed in bfloat16 or wider, within the bound.
No kernel may reach another device: no remote copies, remote signals or barrier semaphores. Data moves between devices by JAX's collectives and lax.ppermute only.
A program may use at most 128 MiB of HBM per device.

v0:
```python
import jax
import jax.numpy as jnp
from jax import lax
from jax.sharding import PartitionSpec as P

inv_temp = 5.0
norm_eps = 1e-06


def swapped(array, axis, distance):
    return lax.ppermute(array, axis, [(i, i ^ 1 << distance) for i in range(lax.axis_size(axis))])


def mix_blocks(ext_blocks, tiles, sources, inv_deg):
    picked = ext_blocks[sources]
    summed = jnp.einsum("ntij,ntjw->niw", tiles, picked, preferred_element_type=jnp.float32)
    own_rows = ext_blocks[: sources.shape[0]].astype(jnp.float32)
    return ((own_rows + summed) * inv_deg[:, :, None]).astype(jnp.bfloat16)


def spread_back(grad_mixed, tiles, sources, inv_deg, total_blocks):
    scaled = (grad_mixed * inv_deg[:, :, None]).astype(jnp.bfloat16)
    spread = jnp.einsum("ntij,niw->ntjw", tiles, scaled, preferred_element_type=jnp.float32)
    ext_grad = jnp.zeros((total_blocks, grad_mixed.shape[1], grad_mixed.shape[2]), jnp.float32)
    ext_grad = ext_grad.at[sources].add(spread)
    return ext_grad.at[: sources.shape[0]].add(scaled.astype(jnp.float32))


def contrast(unit, partner, negatives):
    unit_f = unit.astype(jnp.float32)
    partner_f = partner.astype(jnp.float32)
    positive = inv_temp * jnp.sum(unit_f * partner_f, axis=1)
    scores = inv_temp * jnp.dot(unit, negatives.T, preferred_element_type=jnp.float32)
    expo = jnp.exp(scores)
    total = jnp.exp(positive) + jnp.sum(expo, axis=1)
    node_loss = jnp.log(total) - positive
    prob = (expo / total[:, None]).astype(jnp.bfloat16)
    own_share = jnp.exp(positive) / total
    share_less = own_share - 1.0
    g_anchor = inv_temp * (
        share_less[:, None] * partner_f
        + jnp.dot(prob, negatives, preferred_element_type=jnp.float32)
    )
    g_partner = inv_temp * share_less[:, None] * unit_f
    g_neg = inv_temp * jnp.dot(prob.T, unit, preferred_element_type=jnp.float32)
    return (node_loss, g_anchor, g_partner, g_neg, share_less)


def per_device(
    features, feat_keep, w_first, w_second, adjacency, tile_src, halo_rows, halo_live, neg_pick
):
    row_count, feat_width = features.shape
    hid_width = w_first.shape[1]
    block_rows = adjacency.shape[2]
    block_count = tile_src.shape[1]
    tile_count = tile_src.shape[2]
    part_count = lax.axis_size("dom")
    slot_cap = halo_rows.shape[2]
    neg_count = neg_pick.shape[2]
    tiles = adjacency[0].reshape(block_count, tile_count, block_rows, block_rows)
    sources = tile_src[0]
    inv_deg = 1.0 / (1.0 + jnp.sum(tiles.astype(jnp.float32), axis=(1, 3)))
    keep_cols = feat_keep[0].astype(jnp.bfloat16)
    send_rows = halo_rows[0]
    live_slots = lax.broadcasted_iota(jnp.int32, (part_count, slot_cap), 1) < halo_live[0][:, None]
    live_bf = live_slots.astype(jnp.bfloat16)[:, :, None]
    masked = features * keep_cols
    outgoing = masked[send_rows] * live_bf
    incoming = lax.all_to_all(outgoing, "dom", split_axis=0, concat_axis=0, tiled=True).reshape(
        part_count * slot_cap, feat_width
    )
    ext_first = jnp.concatenate([masked, incoming], 0).reshape(-1, block_rows, feat_width)
    mixed_first = mix_blocks(ext_first, tiles, sources, inv_deg).reshape(row_count, feat_width)
    pre_act = jnp.dot(mixed_first, w_first, preferred_element_type=jnp.float32)
    hidden = jnp.maximum(pre_act, 0.0).astype(jnp.bfloat16)
    hidden_out = hidden[send_rows] * live_bf
    hidden_in = lax.all_to_all(hidden_out, "dom", split_axis=0, concat_axis=0, tiled=True).reshape(
        part_count * slot_cap, hid_width
    )
    ext_second = jnp.concatenate([hidden, hidden_in], 0).reshape(-1, block_rows, hid_width)
    mixed_second = mix_blocks(ext_second, tiles, sources, inv_deg).reshape(row_count, hid_width)
    projected = jnp.dot(mixed_second, w_second, preferred_element_type=jnp.float32)
    inv_norm = lax.rsqrt(jnp.sum(projected * projected, axis=1, keepdims=True) + norm_eps)
    normed = projected * inv_norm
    unit = normed.astype(jnp.bfloat16)
    partner = swapped(unit, "view", 0)
    pick_rows = neg_pick[0].reshape(-1)
    neg_out = partner[neg_pick[0]]
    negatives = lax.all_to_all(neg_out, "dom", split_axis=0, concat_axis=0, tiled=True).reshape(
        part_count * neg_count, hid_width
    )
    node_loss, g_anchor, g_partner, g_neg, share_less = contrast(unit, partner, negatives)
    returned = lax.all_to_all(
        g_neg.reshape(part_count, neg_count, hid_width),
        "dom",
        split_axis=0,
        concat_axis=0,
        tiled=True,
    )
    g_partner = g_partner.at[pick_rows].add(returned.reshape(-1, hid_width))
    g_emb = g_anchor + swapped(g_partner, "view", 0)
    inner = jnp.sum(normed * g_emb, axis=1, keepdims=True)
    g_proj = ((g_emb - normed * inner) * inv_norm).astype(jnp.bfloat16)
    grad_second = jnp.einsum("ih,ik->hk", mixed_second, g_proj, preferred_element_type=jnp.float32)
    g_mixed = jnp.einsum("ik,hk->ih", g_proj, w_second, preferred_element_type=jnp.float32)
    ext_grad = spread_back(
        g_mixed.reshape(block_count, block_rows, hid_width),
        tiles,
        sources,
        inv_deg,
        ext_second.shape[0],
    )
    flat_grad = ext_grad.reshape(-1, hid_width)
    halo_grad = flat_grad[row_count:].reshape(part_count, slot_cap, hid_width)
    back_grad = lax.all_to_all(
        halo_grad.astype(jnp.bfloat16), "dom", split_axis=0, concat_axis=0, tiled=True
    ).astype(halo_grad.dtype)
    back_grad = back_grad * live_slots.astype(jnp.float32)[:, :, None]
    g_hidden = flat_grad[:row_count].at[send_rows.reshape(-1)].add(back_grad.reshape(-1, hid_width))
    g_pre = jnp.where(pre_act > 0, g_hidden, 0.0).astype(jnp.bfloat16)
    grad_first = jnp.einsum("if,ih->fh", mixed_first, g_pre, preferred_element_type=jnp.float32)
    summed = lax.psum((grad_first, grad_second), ("view", "dom"))
    return (node_loss[None, :], summed[0], summed[1])


def solution(mesh):
    placed = (
        P("dom", None),
        P("view", None),
        P(),
        P(),
        P("view", "dom", None, None),
        P("view", "dom", None),
        P("dom", None, None),
        P("dom", None),
        P("dom", None, None),
    )
    return jax.shard_map(
        per_device,
        mesh=mesh,
        in_specs=placed,
        out_specs=(P("view", "dom"), P(), P()),
        check_vma=False,
    )
```

profile of v0, /device:TPU:0, one launch (start us, length us, event | category | flops | bytes accessed | tf_op | source)
XLA Modules:
  0.0 339.7 jit_solution(16240361134284853910)
XLA Ops:
  15.5 8.3 %all-to-all-start = ((bf16[16,8,512]{2,1,0:T(8,128)(2,1)}), bf16[16,8,512]{2,1,0:T(8,128)(2,1)S(1)}, u32[]{:S(2)}, u32[]{:S(2)}) async-start(bf16[16,8,512]{2,1,0:T(8,128)(2,1)} %bitcast_multiply_fusion.1), calls=%async_computation | async-start | bytes 262144 | tf_op jit(solution)/shard_map/all_to_all | solution.py:69
  24.6 7.0 %all-to-all-done = bf16[16,8,512]{2,1,0:T(8,128)(2,1)S(1)} async-done(((bf16[16,8,512]{2,1,0:T(8,128)(2,1)}), bf16[16,8,512]{2,1,0:T(8,128)(2,1)S(1)}, u32[]{:S(2)}, u32[]{:S(2)}) %all-to-all-start) | async-done | bytes 131104 | tf_op jit(solution)/shard_map/all_to_all | solution.py:69
  33.0 5.5 %gather_fusion.1 = bf16[64,128,512]{2,1,0:T(8,128)(2,1)} fusion(bf16[9,128,512]{2,1,0:T(8,128)(2,1)S(1)} %bitcast.105, s32[1024]{0:T(1024)S(1)} %pad_clamp_fusion.1), kind=kCustom, calls=%fused_computation.1 | custom fusion | bytes 16777472 | tf_op jit(solution)/shard_map/gather | solution.py:15
  38.5 5.4 %fusion.7 = bf16[8,128,512]{2,1,0:T(8,128)(2,1)S(1)} fusion(bf16[8,128,512]{2,1,0:T(8,128)(2,1)S(1)} %bitcast.114, bf16[8,8,128,128]{3,2,1,0:T(8,128)(2,1)} %bitcast.107, bf16[8,8,128,512]{3,2,1,0:T(8,128)(2,1)} %bitcast.111, f32[8,128]{1,0:T(8,128)S(1)} %add_divide_fusion), kind=kOutput, calls=%fused_computation.23 | convolution fusion | flops 1075838976 | bytes 12587008 | tf_op jit(solution)/shard_map/ntij,ntjw->niw/dot_general | solution.py:16
  46.9 10.4 %all_to_all.25 = bf16[16,8,512]{2,1,0:T(8,128)(2,1)S(1)} all-to-all(bf16[16,8,512]{2,1,0:T(8,128)(2,1)S(1)} %bitcast_multiply_fusion), channel_id=1, replica_groups=mesh['view'=2,'dom'=16] {'dom'}, dimensions={0} | all-to-all | bytes 262144 | tf_op jit(solution)/shard_map/all_to_all | solution.py:77
  57.3 5.5 %gather_fusion.3 = bf16[64,128,512]{2,1,0:T(8,128)(2,1)} fusion(bf16[9,128,512]{2,1,0:T(8,128)(2,1)S(1)} %bitcast.104, s32[1024]{0:T(1024)S(1)} %pad_clamp_fusion.1), kind=kCustom, calls=%fused_computation.3 | custom fusion | bytes 16777472 | tf_op jit(solution)/shard_map/gather | solution.py:15
  62.9 5.3 %fusion.5 = bf16[8,128,512]{2,1,0:T(8,128)(2,1)S(1)} fusion(bf16[8,128,512]{2,1,0:T(8,128)(2,1)S(1)} %bitcast.115, bf16[8,8,128,128]{3,2,1,0:T(8,128)(2,1)} %bitcast.108, bf16[8,8,128,512]{3,2,1,0:T(8,128)(2,1)} %bitcast.110, f32[8,128]{1,0:T(8,128)S(1)} %add_divide_fusion), kind=kOutput, calls=%fused_computation.20 | convolution fusion | flops 1075838976 | bytes 12587008 | tf_op jit(solution)/shard_map/ntij,ntjw->niw/dot_general | solution.py:16
  78.4 3.5 %all-to-all-start.2 = ((bf16[16,8,512]{2,1,0:T(8,128)(2,1)}), bf16[16,8,512]{2,1,0:T(8,128)(2,1)S(1)}, u32[]{:S(2)}, u32[]{:S(2)}) async-start(bf16[16,8,512]{2,1,0:T(8,128)(2,1)} %bitcast.25), calls=%async_computation.2 | async-start | bytes 262144 | tf_op jit(solution)/shard_map/all_to_all | solution.py:89
  84.2 5.7 %all-to-all-done.2 = bf16[16,8,512]{2,1,0:T(8,128)(2,1)S(1)} async-done(((bf16[16,8,512]{2,1,0:T(8,128)(2,1)}), bf16[16,8,512]{2,1,0:T(8,128)(2,1)S(1)}, u32[]{:S(2)}, u32[]{:S(2)}) %all-to-all-start.2) | async-done | bytes 131104 | tf_op jit(solution)/shard_map/all_to_all | solution.py:89
  94.5 3.7 %all-to-all-start.3 = ((f32[16,8,512]{2,1,0:T(8,128)}), f32[16,8,512]{2,1,0:T(8,128)S(1)}, u32[]{:S(2)}, u32[]{:S(2)}) async-start(f32[16,8,512]{2,1,0:T(8,128)} %fusion.9), calls=%async_computation.3 | async-start | bytes 524288 | tf_op jit(solution)/shard_map/all_to_all | solution.py:93
  101.7 2.9 copy.33
  107.4 4.4 %scatter_custom_fusion = f32[1024,512]{1,0:T(8,128)} fusion(f32[1024,512]{1,0:T(8,128)} %copy.33, s32[128]{0:T(128)} %fusion.28, f32[16,8,512]{2,1,0:T(8,128)S(1)} %all-to-all-done.3), kind=kCustom, calls=%fused_computation.45 | custom fusion | flops 65536 | bytes 2359296 | tf_op jit(solution)/shard_map/scatter-add | solution.py:100
  111.7 2.9 copy.34
  114.8 4.3 %collective-permute-done.1 = f32[1024,512]{0,1:T(8,128)} collective-permute-done((f32[1024,512]{0,1:T(8,128)}, f32[1024,512]{0,1:T(8,128)}, u32[]{:S(2)}, u32[]{:S(2)}) %collective-permute-start.1) | collective-permute-done | bytes 2097184 | tf_op jit(solution)/shard_map/ppermute | solution.py:11
  125.4 8.2 %convolution_bitcast_fusion = f32[8,8,128,512]{2,3,1,0:T(8,128)} fusion(bf16[8,8,128,128]{3,2,1,0:T(8,128)(2,1)S(1)} %bitcast.109, f32[8,128,512]{2,1,0:T(8,128)S(1)} %bitcast.112, f32[8,128]{1,0:T(8,128)S(1)} %add_divide_fusion), kind=kOutput, calls=%fused_computation.8 | convolution fusion | flops 1074790400 | bytes 20975616 | tf_op jit(solution)/shard_map/ntij,niw->ntjw/dot_general | solution.py:23
  133.6 16.5 %copy.36 = f32[8,8,128,512]{3,2,1,0:T(8,128)} copy(f32[8,8,128,512]{2,3,1,0:T(8,128)} %convolution_bitcast_fusion) | data formatting | bytes 33554432 | tf_op jit(solution)/shard_map/ntij,niw->ntjw/dot_general | solution.py:23
  150.3 23.0 %scatter_fusion = f32[9,128,512]{2,1,0:T(8,128)S(1)} fusion(f32[9,128,512]{2,1,0:T(8,128)S(1)} %broadcast_in_dim.3, s32[64]{0:T(128)S(1)} %reshape.345, f32[64,128,512]{2,1,0:T(8,128)} %bitcast.106), kind=kCustom, calls=%fused_computation.6 | custom fusion | flops 4194304 | bytes 50331904 | tf_op jit(solution)/shard_map/scatter-add | solution.py:25
  173.4 3.2 slice_add_fusion
  177.3 3.9 %all-to-all-start.4 = ((bf16[16,8,512]{2,1,0:T(8,128)(2,1)}), bf16[16,8,512]{2,1,0:T(8,128)(2,1)S(1)}, u32[]{:S(2)}, u32[]{:S(2)}) async-start(bf16[16,8,512]{2,1,0:T(8,128)(2,1)} %fusion.19), calls=%async_computation.4 | async-start | bytes 262144 | tf_op jit(solution)/shard_map/all_to_all | solution.py:115
  181.2 3.3 fusion.33
  184.6 4.4 %all-to-all-done.4 = bf16[16,8,512]{2,1,0:T(8,128)(2,1)S(1)} async-done(((bf16[16,8,512]{2,1,0:T(8,128)(2,1)}), bf16[16,8,512]{2,1,0:T(8,128)(2,1)S(1)}, u32[]{:S(2)}, u32[]{:S(2)}) %all-to-all-start.4) | async-done | bytes 131104 | tf_op jit(solution)/shard_map/all_to_all | solution.py:115
  189.0 4.3 %scatter_custom_fusion.2 = f32[1024,512]{1,0:T(8,128)} fusion(f32[1024,512]{1,0:T(8,128)} %bitcast.118, s32[128]{0:T(128)S(1)} %fusion.29, bf16[16,8,512]{2,1,0:T(8,128)(2,1)S(1)} %all-to-all-done.4, f32[16,8]{1,0:T(8,128)S(1)} %copy-done.12), kind=kCustom, calls=%fused_computation.43 | custom fusion | flops 196608 | bytes 2236416 | tf_op jit(solution)/shard_map/scatter-add | solution.py:119
  193.3 3.9 %fusion.10 = f32[512,512]{1,0:T(8,128)} fusion(bf16[1024,512]{1,0:T(8,128)(2,1)S(1)} %bitcast.117, f32[1024,512]{1,0:T(8,128)} %scatter_custom_fusion.2, f32[1024,512]{1,0:T(8,128)} %get-tuple-element.24), kind=kOutput, calls=%fused_computation.37 | convolution fusion | flops 537919488 | bytes 6291456 | tf_op jit(solution)/shard_map/if,ih->fh/dot_general | solution.py:121
  198.5 131.0 %all-reduce.3.cloned.1.call-done = (f32[512,512]{1,0:T(8,128)}, f32[512,512]{1,0:T(8,128)}) async-done(((f32[512,512]{1,0:T(8,128)}, f32[512,512]{1,0:T(8,128)}), (f32[512,512]{1,0:T(8,128)}, f32[512,512]{1,0:T(8,128)})) %all-reduce.3.cloned.1.call-update) | async-done | bytes 2097168 | tf_op jit(solution)/shard_map/psum | solution.py:122
  (94 shorter events, 48.7 us)
Async XLA Ops:
  7.2 61.0 %copy-start = (bf16[512,512]{1,0:T(8,128)(2,1)S(1)}, bf16[512,512]{1,0:T(8,128)(2,1)}, u32[]{:S(2)}) copy-start(bf16[512,512]{1,0:T(8,128)(2,1)} %param.14) | copy-start | bytes 1572868
  7.2 16.7 %copy-start.19 = (s32[1,8,8]{2,1,0:T(8,128)S(1)}, s32[1,8,8]{2,1,0:T(8,128)}, u32[]{:S(2)}) copy-start(s32[1,8,8]{2,1,0:T(8,128)} %param.16) | copy-start | bytes 772
  7.2 16.8 %copy-start.2 = (bf16[1,64,128,128]{3,2,1,0:T(8,128)(2,1)S(1)}, bf16[1,64,128,128]{3,2,1,0:T(8,128)(2,1)}, u32[]{:S(2)}) copy-start(bf16[1,64,128,128]{3,2,1,0:T(8,128)(2,1)} %param.15) | copy-start | bytes 6291460
  15.5 16.1 %all-to-all-start = ((bf16[16,8,512]{2,1,0:T(8,128)(2,1)}), bf16[16,8,512]{2,1,0:T(8,128)(2,1)S(1)}, u32[]{:S(2)}, u32[]{:S(2)}) async-start(bf16[16,8,512]{2,1,0:T(8,128)(2,1)} %bitcast_multiply_fusion.1), calls=%async_computation | async-start | bytes 262144 | tf_op jit(solution)/shard_map/all_to_all | solution.py:69
  32.9 5.5 %copy-start.5 = (bf16[1024,512]{1,0:T(8,128)(2,1)S(1)}, bf16[1024,512]{1,0:T(8,128)(2,1)}, u32[]{:S(2)}) copy-start(bf16[1024,512]{1,0:T(8,128)(2,1)} %broadcast_multiply_fusion) | copy-start | bytes 3145732
  38.5 5.4 %copy-start.11 = (bf16[512,512]{1,0:T(8,128)(2,1)S(1)}, bf16[512,512]{1,0:T(8,128)(2,1)}, u32[]{:S(2)}) copy-start(bf16[512,512]{1,0:T(8,128)(2,1)} %param.13) | copy-start | bytes 1572868
  43.8 2.1 copy-start.6
  68.2 2.1 copy-start.8
  70.2 3.0 collective-permute-start
  78.4 11.5 %all-to-all-start.2 = ((bf16[16,8,512]{2,1,0:T(8,128)(2,1)}), bf16[16,8,512]{2,1,0:T(8,128)(2,1)S(1)}, u32[]{:S(2)}, u32[]{:S(2)}) async-start(bf16[16,8,512]{2,1,0:T(8,128)(2,1)} %bitcast.25), calls=%async_computation.2 | async-start | bytes 262144 | tf_op jit(solution)/shard_map/all_to_all | solution.py:89
  92.1 2.4 copy-start.14
  94.5 12.8 %all-to-all-start.3 = ((f32[16,8,512]{2,1,0:T(8,128)}), f32[16,8,512]{2,1,0:T(8,128)S(1)}, u32[]{:S(2)}, u32[]{:S(2)}) async-start(f32[16,8,512]{2,1,0:T(8,128)} %fusion.9), calls=%async_computation.3 | async-start | bytes 524288 | tf_op jit(solution)/shard_map/all_to_all | solution.py:93
  111.7 2.9 copy-start.17
  111.7 7.4 %copy-start.13 = (f32[1024]{0:T(1024)S(1)}, f32[1024]{0:T(1024)}, u32[]{:S(2)}) copy-start(f32[1024]{0:T(1024)} %get-tuple-element.18) | copy-start | bytes 12292
  111.7 7.4 %copy-start.15 = (f32[1024]{0:T(1024)S(1)}, f32[1024]{0:T(1024)}, u32[]{:S(2)}) copy-start(f32[1024]{0:T(1024)} %copy-done.14) | copy-start | bytes 12292
  114.6 4.5 %collective-permute-start.1 = (f32[1024,512]{0,1:T(8,128)}, f32[1024,512]{0,1:T(8,128)}, u32[]{:S(2)}, u32[]{:S(2)}) collective-permute-start(f32[1024,512]{0,1:T(8,128)} %copy.34), channel_id=1, source_target_pairs={{0,16},{16,0},{1,17},{17,1},{2,18},{18,2},{3,19},{19,3},{4,20},{20... | collective-permute-start | bytes 6291464 | tf_op jit(solution)/shard_map/ppermute | solution.py:11
  123.3 2.2 copy-start.3
  124.0 1.4 copy-start.4
  176.6 12.4 %copy-start.12 = (f32[16,8]{1,0:T(8,128)S(1)}, f32[16,8]{1,0:T(8,128)}, u32[]{:S(2)}) copy-start(f32[16,8]{1,0:T(8,128)} %get-tuple-element.21) | copy-start | bytes 1540
  177.3 11.7 %all-to-all-start.4 = ((bf16[16,8,512]{2,1,0:T(8,128)(2,1)}), bf16[16,8,512]{2,1,0:T(8,128)(2,1)S(1)}, u32[]{:S(2)}, u32[]{:S(2)}) async-start(bf16[16,8,512]{2,1,0:T(8,128)(2,1)} %fusion.19), calls=%async_computation.4 | async-start | bytes 262144 | tf_op jit(solution)/shard_map/all_to_all | solution.py:115
  181.2 12.1 %copy-start.7 = (bf16[8,128,512]{2,1,0:T(8,128)(2,1)S(1)}, bf16[8,128,512]{2,1,0:T(8,128)(2,1)}, u32[]{:S(2)}) copy-start(bf16[8,128,512]{2,1,0:T(8,128)(2,1)} %copy-done.6) | copy-start | bytes 3145732
  181.2 148.3 %all-reduce.3.cloned.1.call-start = ((), (), s32[]{:S(2)}) async-start(), calls=%async_computation.5 | async-start | bytes 4194304 | tf_op jit(solution)/shard_map/psum | solution.py:122
  329.5 2.4 copy-start.10
  329.5 3.4 copy-start.1
  (3 other events, 2.9 us)
Sparse Core Ops, SparseCore 0:
  197.3 132.1 all-reduce.2
where the time goes:
time: 341 us; the launch traced here: 340 us
  waiting for transfers between devices  158 us (46%)
  other arithmetic  50.9 us (15%)
  local copies, waits for them, and re-layouts  50.3 us (15%)
  matrix products  36.3 us (11%)
  starting transfers between devices  19.5 us (6%)
  between operations  14.4 us (4%)
  blocking collectives  10.4 us (3%)
    psum x1, waiting for transfers between devices, per_device(): summed = lax.psum((grad_first, grad_second), ('view', 'dom'))  131 us
    scatter-add x1, other arithmetic, spread_back(): ext_grad = ext_grad.at[sources].add(spread)  23 us
    dot_general x1, local copies, waits for them, and re-layouts, spread_back(): jnp.einsum('ntij,niw->ntjw', tiles, scaled, preferred_element_type=jnp.fl...  16.5 us
    gather x2, local copies, waits for them, and re-layouts, mix_blocks(): picked = ext_blocks[sources]  11.1 us
    dot_general x2, matrix products, mix_blocks(): jnp.einsum('ntij,ntjw->niw', tiles, picked, preferred_element_type=jnp.fl...  10.7 us
    all_to_all x1, blocking collectives, per_device(): lax.all_to_all(hidden_out, 'dom', split_axis=0, concat_axis=0, tiled=True)  10.4 us
    all_to_all x1, starting transfers between devices, per_device(): lax.all_to_all(outgoing, 'dom', split_axis=0, concat_axis=0, tiled=True)  8.34 us
    dot_general x1, matrix products, spread_back(): jnp.einsum('ntij,niw->ntjw', tiles, scaled, preferred_element_type=jnp.fl...  8.17 us
  transfers between devices with their start and end apart: 7, of which 7 were waited for; matrix products, arithmetic and copies ran while one was open for 4% of the time, Pallas kernels for 0%

commit v1 on v0

--- a/solution.py
+++ b/solution.py
@@ -119,7 +119,7 @@
     g_hidden = flat_grad[:row_count].at[send_rows.reshape(-1)].add(back_grad.reshape(-1, hid_width))
     g_pre = jnp.where(pre_act > 0, g_hidden, 0.0).astype(jnp.bfloat16)
     grad_first = jnp.einsum("if,ih->fh", mixed_first, g_pre, preferred_element_type=jnp.float32)
-    summed = lax.psum((grad_first, grad_second), ("view", "dom"))
+    summed = lax.psum(lax.psum((grad_first, grad_second), "view"), "dom")
     return (node_loss[None, :], summed[0], summed[1])
 
 

time: 341 us -> 361 us (1.059)
  waiting for transfers between devices: 158 us -> 179 us
    psum x1 -> x2, waiting for transfers between devices: 131 us -> 152 us  [per_device(): summed = lax.psum(lax.psum((grad_first, grad_second), 'view'), 'dom')]
  transfers between devices with their start and end apart: 7 -> 8, of which waited for: 7 -> 8; matrix products, arithmetic and copies ran while one was open for 4% -> 4% of each run, Pallas kernels for 0% -> 0%
where the time goes in v1:
time: 361 us; the launch traced here: 360 us
  waiting for transfers between devices  179 us (50%)
  other arithmetic  50.9 us (14%)
  local copies, waits for them, and re-layouts  49.6 us (14%)
  matrix products  36.3 us (10%)
  starting transfers between devices  19.6 us (5%)
  between operations  14.4 us (4%)
  blocking collectives  10.4 us (3%)
    psum x2, waiting for transfers between devices, per_device(): summed = lax.psum(lax.psum((grad_first, grad_second), 'view'), 'dom')  152 us
    scatter-add x1, other arithmetic, spread_back(): ext_grad = ext_grad.at[sources].add(spread)  23 us
    dot_general x1, local copies, waits for them, and re-layouts, spread_back(): jnp.einsum('ntij,niw->ntjw', tiles, scaled, preferred_element_type=jnp.fl...  16.5 us
    gather x2, local copies, waits for them, and re-layouts, mix_blocks(): picked = ext_blocks[sources]  11 us
    dot_general x2, matrix products, mix_blocks(): jnp.einsum('ntij,ntjw->niw', tiles, picked, preferred_element_type=jnp.fl...  10.6 us
    all_to_all x1, blocking collectives, per_device(): lax.all_to_all(hidden_out, 'dom', split_axis=0, concat_axis=0, tiled=True)  10.4 us
    all_to_all x1, starting transfers between devices, per_device(): lax.all_to_all(outgoing, 'dom', split_axis=0, concat_axis=0, tiled=True)  8.34 us
    dot_general x1, matrix products, spread_back(): jnp.einsum('ntij,niw->ntjw', tiles, scaled, preferred_element_type=jnp.fl...  8.19 us
  transfers between devices with their start and end apart: 8, of which 8 were waited for; matrix products, arithmetic and copies ran while one was open for 4% of the time, Pallas kernels for 0%

profile of v1, /device:TPU:0, one launch (start us, length us, event | category | flops | bytes accessed | tf_op | source)
XLA Modules:
  0.0 359.9 jit_solution(5992195882639328221)
XLA Ops:
  15.5 8.3 %all-to-all-start = ((bf16[16,8,512]{2,1,0:T(8,128)(2,1)}), bf16[16,8,512]{2,1,0:T(8,128)(2,1)S(1)}, u32[]{:S(2)}, u32[]{:S(2)}) async-start(bf16[16,8,512]{2,1,0:T(8,128)(2,1)} %bitcast_multiply_fusion.1), calls=%async_computation | async-start | bytes 262144 | tf_op jit(solution)/shard_map/all_to_all | solution.py:69
  24.6 7.0 %all-to-all-done = bf16[16,8,512]{2,1,0:T(8,128)(2,1)S(1)} async-done(((bf16[16,8,512]{2,1,0:T(8,128)(2,1)}), bf16[16,8,512]{2,1,0:T(8,128)(2,1)S(1)}, u32[]{:S(2)}, u32[]{:S(2)}) %all-to-all-start) | async-done | bytes 131104 | tf_op jit(solution)/shard_map/all_to_all | solution.py:69
  33.0 5.5 %gather_fusion.1 = bf16[64,128,512]{2,1,0:T(8,128)(2,1)} fusion(bf16[9,128,512]{2,1,0:T(8,128)(2,1)S(1)} %bitcast.105, s32[1024]{0:T(1024)S(1)} %pad_clamp_fusion.1), kind=kCustom, calls=%fused_computation.1 | custom fusion | bytes 16777472 | tf_op jit(solution)/shard_map/gather | solution.py:15
  38.5 5.3 %fusion.7 = bf16[8,128,512]{2,1,0:T(8,128)(2,1)S(1)} fusion(bf16[8,128,512]{2,1,0:T(8,128)(2,1)S(1)} %bitcast.114, bf16[8,8,128,128]{3,2,1,0:T(8,128)(2,1)} %bitcast.107, bf16[8,8,128,512]{3,2,1,0:T(8,128)(2,1)} %bitcast.111, f32[8,128]{1,0:T(8,128)S(1)} %add_divide_fusion), kind=kOutput, calls=%fused_computation.23 | convolution fusion | flops 1075838976 | bytes 12587008 | tf_op jit(solution)/shard_map/ntij,ntjw->niw/dot_general | solution.py:16
  46.8 10.4 %all_to_all.25 = bf16[16,8,512]{2,1,0:T(8,128)(2,1)S(1)} all-to-all(bf16[16,8,512]{2,1,0:T(8,128)(2,1)S(1)} %bitcast_multiply_fusion), channel_id=1, replica_groups=mesh['view'=2,'dom'=16] {'dom'}, dimensions={0} | all-to-all | bytes 262144 | tf_op jit(solution)/shard_map/all_to_all | solution.py:77
  57.3 5.5 %gather_fusion.3 = bf16[64,128,512]{2,1,0:T(8,128)(2,1)} fusion(bf16[9,128,512]{2,1,0:T(8,128)(2,1)S(1)} %bitcast.104, s32[1024]{0:T(1024)S(1)} %pad_clamp_fusion.1), kind=kCustom, calls=%fused_computation.3 | custom fusion | bytes 16777472 | tf_op jit(solution)/shard_map/gather | solution.py:15
  62.8 5.3 %fusion.5 = bf16[8,128,512]{2,1,0:T(8,128)(2,1)S(1)} fusion(bf16[8,128,512]{2,1,0:T(8,128)(2,1)S(1)} %bitcast.115, bf16[8,8,128,128]{3,2,1,0:T(8,128)(2,1)} %bitcast.108, bf16[8,8,128,512]{3,2,1,0:T(8,128)(2,1)} %bitcast.110, f32[8,128]{1,0:T(8,128)S(1)} %add_divide_fusion), kind=kOutput, calls=%fused_computation.20 | convolution fusion | flops 1075838976 | bytes 12587008 | tf_op jit(solution)/shard_map/ntij,ntjw->niw/dot_general | solution.py:16
  78.4 3.5 all-to-all-start.2
  84.2 5.7 %all-to-all-done.2 = bf16[16,8,512]{2,1,0:T(8,128)(2,1)S(1)} async-done(((bf16[16,8,512]{2,1,0:T(8,128)(2,1)}), bf16[16,8,512]{2,1,0:T(8,128)(2,1)S(1)}, u32[]{:S(2)}, u32[]{:S(2)}) %all-to-all-start.2) | async-done | bytes 131104 | tf_op jit(solution)/shard_map/all_to_all | solution.py:89
  94.5 3.7 %all-to-all-start.3 = ((f32[16,8,512]{2,1,0:T(8,128)}), f32[16,8,512]{2,1,0:T(8,128)S(1)}, u32[]{:S(2)}, u32[]{:S(2)}) async-start(f32[16,8,512]{2,1,0:T(8,128)} %fusion.9), calls=%async_computation.3 | async-start | bytes 524288 | tf_op jit(solution)/shard_map/all_to_all | solution.py:93
  101.6 2.9 copy.33
  107.3 4.3 %scatter_custom_fusion = f32[1024,512]{1,0:T(8,128)} fusion(f32[1024,512]{1,0:T(8,128)} %copy.33, s32[128]{0:T(128)} %fusion.28, f32[16,8,512]{2,1,0:T(8,128)S(1)} %all-to-all-done.3), kind=kCustom, calls=%fused_computation.45 | custom fusion | flops 65536 | bytes 2359296 | tf_op jit(solution)/shard_map/scatter-add | solution.py:100
  114.8 4.3 %collective-permute-done.1 = f32[1024,512]{0,1:T(8,128)} collective-permute-done((f32[1024,512]{0,1:T(8,128)}, f32[1024,512]{0,1:T(8,128)}, u32[]{:S(2)}, u32[]{:S(2)}) %collective-permute-start.1) | collective-permute-done | bytes 2097184 | tf_op jit(solution)/shard_map/ppermute | solution.py:11
  125.4 8.2 %convolution_bitcast_fusion = f32[8,8,128,512]{2,3,1,0:T(8,128)} fusion(bf16[8,8,128,128]{3,2,1,0:T(8,128)(2,1)S(1)} %bitcast.109, f32[8,128,512]{2,1,0:T(8,128)S(1)} %bitcast.112, f32[8,128]{1,0:T(8,128)S(1)} %add_divide_fusion), kind=kOutput, calls=%fused_computation.8 | convolution fusion | flops 1074790400 | bytes 20975616 | tf_op jit(solution)/shard_map/ntij,niw->ntjw/dot_general | solution.py:23
  133.6 16.5 %copy.36 = f32[8,8,128,512]{3,2,1,0:T(8,128)} copy(f32[8,8,128,512]{2,3,1,0:T(8,128)} %convolution_bitcast_fusion) | data formatting | bytes 33554432 | tf_op jit(solution)/shard_map/ntij,niw->ntjw/dot_general | solution.py:23
  150.3 23.0 %scatter_fusion = f32[9,128,512]{2,1,0:T(8,128)S(1)} fusion(f32[9,128,512]{2,1,0:T(8,128)S(1)} %broadcast_in_dim.3, s32[64]{0:T(128)S(1)} %reshape.345, f32[64,128,512]{2,1,0:T(8,128)} %bitcast.106), kind=kCustom, calls=%fused_computation.6 | custom fusion | flops 4194304 | bytes 50331904 | tf_op jit(solution)/shard_map/scatter-add | solution.py:25
  173.4 3.2 slice_add_fusion
  177.2 3.9 %all-to-all-start.4 = ((bf16[16,8,512]{2,1,0:T(8,128)(2,1)}), bf16[16,8,512]{2,1,0:T(8,128)(2,1)S(1)}, u32[]{:S(2)}, u32[]{:S(2)}) async-start(bf16[16,8,512]{2,1,0:T(8,128)(2,1)} %fusion.19), calls=%async_computation.4 | async-start | bytes 262144 | tf_op jit(solution)/shard_map/all_to_all | solution.py:115
  181.2 3.3 fusion.33
  184.5 4.4 %all-to-all-done.4 = bf16[16,8,512]{2,1,0:T(8,128)(2,1)S(1)} async-done(((bf16[16,8,512]{2,1,0:T(8,128)(2,1)}), bf16[16,8,512]{2,1,0:T(8,128)(2,1)S(1)}, u32[]{:S(2)}, u32[]{:S(2)}) %all-to-all-start.4) | async-done | bytes 131104 | tf_op jit(solution)/shard_map/all_to_all | solution.py:115
  188.9 4.3 %scatter_custom_fusion.2 = f32[1024,512]{1,0:T(8,128)} fusion(f32[1024,512]{1,0:T(8,128)} %bitcast.118, s32[128]{0:T(128)S(1)} %fusion.29, bf16[16,8,512]{2,1,0:T(8,128)(2,1)S(1)} %all-to-all-done.4, f32[16,8]{1,0:T(8,128)S(1)} %copy-done.12), kind=kCustom, calls=%fused_computation.43 | custom fusion | flops 196608 | bytes 2236416 | tf_op jit(solution)/shard_map/scatter-add | solution.py:119
  193.2 3.9 %fusion.10 = f32[512,512]{1,0:T(8,128)} fusion(bf16[1024,512]{1,0:T(8,128)(2,1)S(1)} %bitcast.117, f32[1024,512]{1,0:T(8,128)} %scatter_custom_fusion.2, f32[1024,512]{1,0:T(8,128)} %get-tuple-element.26), kind=kOutput, calls=%fused_computation.37 | convolution fusion | flops 537919488 | bytes 6291456 | tf_op jit(solution)/shard_map/if,ih->fh/dot_general | solution.py:121
  197.2 19.0 %all-reduce.7.cloned.1.call-done = (f32[512,512]{1,0:T(8,128)}, f32[512,512]{1,0:T(8,128)}) async-done(((f32[512,512]{1,0:T(8,128)}, f32[512,512]{1,0:T(8,128)}), (f32[512,512]{1,0:T(8,128)}, f32[512,512]{1,0:T(8,128)})) %all-reduce.7.cloned.1.call-update) | async-done | bytes 2097168 | tf_op jit(solution)/shard_map/psum | solution.py:122
  216.9 132.8 %all-reduce.5.cloned.1.call-done = (f32[512,512]{1,0:T(8,128)}, f32[512,512]{1,0:T(8,128)}) async-done(((f32[512,512]{1,0:T(8,128)}, f32[512,512]{1,0:T(8,128)}), (f32[512,512]{1,0:T(8,128)}, f32[512,512]{1,0:T(8,128)})) %all-reduce.5.cloned.1.call-update) | async-done | bytes 2097168 | tf_op jit(solution)/shard_map/psum | solution.py:122
  (97 shorter events, 51.0 us)
Async XLA Ops:
  7.2 61.0 %copy-start = (bf16[512,512]{1,0:T(8,128)(2,1)S(1)}, bf16[512,512]{1,0:T(8,128)(2,1)}, u32[]{:S(2)}) copy-start(bf16[512,512]{1,0:T(8,128)(2,1)} %param.14) | copy-start | bytes 1572868
  7.2 16.7 %copy-start.19 = (s32[1,8,8]{2,1,0:T(8,128)S(1)}, s32[1,8,8]{2,1,0:T(8,128)}, u32[]{:S(2)}) copy-start(s32[1,8,8]{2,1,0:T(8,128)} %param.16) | copy-start | bytes 772
  7.2 16.8 %copy-start.2 = (bf16[1,64,128,128]{3,2,1,0:T(8,128)(2,1)S(1)}, bf16[1,64,128,128]{3,2,1,0:T(8,128)(2,1)}, u32[]{:S(2)}) copy-start(bf16[1,64,128,128]{3,2,1,0:T(8,128)(2,1)} %param.15) | copy-start | bytes 6291460
  15.5 16.1 %all-to-all-start = ((bf16[16,8,512]{2,1,0:T(8,128)(2,1)}), bf16[16,8,512]{2,1,0:T(8,128)(2,1)S(1)}, u32[]{:S(2)}, u32[]{:S(2)}) async-start(bf16[16,8,512]{2,1,0:T(8,128)(2,1)} %bitcast_multiply_fusion.1), calls=%async_computation | async-start | bytes 262144 | tf_op jit(solution)/shard_map/all_to_all | solution.py:69
  32.9 5.5 %copy-start.5 = (bf16[1024,512]{1,0:T(8,128)(2,1)S(1)}, bf16[1024,512]{1,0:T(8,128)(2,1)}, u32[]{:S(2)}) copy-start(bf16[1024,512]{1,0:T(8,128)(2,1)} %broadcast_multiply_fusion) | copy-start | bytes 3145732
  38.5 5.4 %copy-start.11 = (bf16[512,512]{1,0:T(8,128)(2,1)S(1)}, bf16[512,512]{1,0:T(8,128)(2,1)}, u32[]{:S(2)}) copy-start(bf16[512,512]{1,0:T(8,128)(2,1)} %param.13) | copy-start | bytes 1572868
  43.8 2.1 copy-start.6
  70.2 3.0 collective-permute-start
  78.4 11.5 %all-to-all-start.2 = ((bf16[16,8,512]{2,1,0:T(8,128)(2,1)}), bf16[16,8,512]{2,1,0:T(8,128)(2,1)S(1)}, u32[]{:S(2)}, u32[]{:S(2)}) async-start(bf16[16,8,512]{2,1,0:T(8,128)(2,1)} %bitcast.25), calls=%async_computation.2 | async-start | bytes 262144 | tf_op jit(solution)/shard_map/all_to_all | solution.py:89
  92.0 2.4 copy-start.14
  94.5 12.8 %all-to-all-start.3 = ((f32[16,8,512]{2,1,0:T(8,128)}), f32[16,8,512]{2,1,0:T(8,128)S(1)}, u32[]{:S(2)}, u32[]{:S(2)}) async-start(f32[16,8,512]{2,1,0:T(8,128)} %fusion.9), calls=%async_computation.3 | async-start | bytes 524288 | tf_op jit(solution)/shard_map/all_to_all | solution.py:93
  111.7 2.9 copy-start.17
  111.7 7.4 %copy-start.13 = (f32[1024]{0:T(1024)S(1)}, f32[1024]{0:T(1024)}, u32[]{:S(2)}) copy-start(f32[1024]{0:T(1024)} %get-tuple-element.20) | copy-start | bytes 12292
  111.7 7.4 %copy-start.15 = (f32[1024]{0:T(1024)S(1)}, f32[1024]{0:T(1024)}, u32[]{:S(2)}) copy-start(f32[1024]{0:T(1024)} %copy-done.14) | copy-start | bytes 12292
  114.6 4.5 %collective-permute-start.1 = (f32[1024,512]{0,1:T(8,128)}, f32[1024,512]{0,1:T(8,128)}, u32[]{:S(2)}, u32[]{:S(2)}) collective-permute-start(f32[1024,512]{0,1:T(8,128)} %copy.34), channel_id=1, source_target_pairs={{0,16},{16,0},{1,17},{17,1},{2,18},{18,2},{3,19},{19,3},{4,20},{20... | collective-permute-start | bytes 6291464 | tf_op jit(solution)/shard_map/ppermute | solution.py:11
  123.2 2.2 copy-start.3
  176.6 12.4 %copy-start.12 = (f32[16,8]{1,0:T(8,128)S(1)}, f32[16,8]{1,0:T(8,128)}, u32[]{:S(2)}) copy-start(f32[16,8]{1,0:T(8,128)} %get-tuple-element.23) | copy-start | bytes 1540
  177.2 11.7 %all-to-all-start.4 = ((bf16[16,8,512]{2,1,0:T(8,128)(2,1)}), bf16[16,8,512]{2,1,0:T(8,128)(2,1)S(1)}, u32[]{:S(2)}, u32[]{:S(2)}) async-start(bf16[16,8,512]{2,1,0:T(8,128)(2,1)} %fusion.19), calls=%async_computation.4 | async-start | bytes 262144 | tf_op jit(solution)/shard_map/all_to_all | solution.py:115
  181.1 12.1 %copy-start.7 = (bf16[8,128,512]{2,1,0:T(8,128)(2,1)S(1)}, bf16[8,128,512]{2,1,0:T(8,128)(2,1)}, u32[]{:S(2)}) copy-start(bf16[8,128,512]{2,1,0:T(8,128)(2,1)} %copy-done.6) | copy-start | bytes 3145732
  181.1 35.1 %all-reduce.7.cloned.1.call-start = ((), (), s32[]{:S(2)}) async-start(), calls=%async_computation.6 | async-start | bytes 4194304 | tf_op jit(solution)/shard_map/psum | solution.py:122
  197.2 19.1 %copy-start.18 = (f32[1024]{0:T(1024)S(1)}, f32[1024]{0:T(1024)}, u32[]{:S(2)}) copy-start(f32[1024]{0:T(1024)} %get-tuple-element.22) | copy-start | bytes 12292
  197.2 152.5 %all-reduce.5.cloned.1.call-start = ((), (), s32[]{:S(2)}) async-start(), calls=%async_computation.5 | async-start | bytes 4194304 | tf_op jit(solution)/shard_map/psum | solution.py:122
  349.7 2.4 copy-start.10
  349.7 3.4 copy-start.1
  (4 other events, 5.7 us)
Sparse Core Ops, SparseCore 0:
  197.3 18.9 all-reduce.6
  221.8 127.8 all-reduce.4
